TPU v7x, 512 devices: a whole 4x4x16 slice. The times are simulated.
512 devices in a mesh: row: 8 (over x, core), col: 16 (over z), layer: 4 (over y).
Axes of the slice: x: 4, y: 4, z: 16, core: 2. Of those that a mesh axis runs over, the one named last changes fastest.
Arguments:
- occurrences: bfloat16 [8192, 10240], P(('row', 'col', 'layer')), may hold values from -6 to 6
- idf_weight: float32 [8192], P(('row', 'col', 'layer')), may hold values from 0.25 to 2
- pattern: int32 [64, 80], replicated, may hold values 0 or 1
Outputs:
- margin: bfloat16 [10240, 10240], P('row', 'col')
All inputs are finite; a program needn't handle non-finite values.
Results may differ from a plain program's by a relative error of at most 0.0058.
Values may be sent and summed in bfloat16 or wider, within the bound.
No kernel may reach another device: no remote copies, remote signals or barrier semaphores. Data moves between devices by JAX's collectives and lax.ppermute only.
A program may use at most 64 MiB of HBM per device.

v0:
```python
import math
import jax
import jax.numpy as jnp
from jax import lax
from jax.sharding import PartitionSpec as P


def finish(partial_rows, row_start, col_start, factor):
    row_ids = row_start + lax.broadcasted_iota(jnp.int32, partial_rows.shape, 0)
    col_ids = col_start + lax.broadcasted_iota(jnp.int32, partial_rows.shape, 1)
    result = jnp.where(row_ids == col_ids, jnp.float32(0.0), partial_rows * factor)
    return result.astype(jnp.bfloat16)


def body(occurrences, idf_weight, pattern):
    owned, reads = occurrences.shape
    n_rows = lax.axis_size("row")
    n_cols = lax.axis_size("col")
    n_layers = lax.axis_size("layer")
    factor = 1.0 / math.sqrt(owned * n_rows * n_cols * n_layers)
    owner = lax.axis_index(("row", "col", "layer"))
    block_row = owner * owned // 128
    flags = lax.dynamic_slice_in_dim(pattern, block_row, 1, 0)[0]
    read_mask = jnp.repeat(flags.astype(jnp.float32), 128)
    weighted = (occurrences.astype(jnp.float32) * idf_weight[:, None] * read_mask[None, :]).astype(
        jnp.bfloat16
    )
    piece_len = reads // (n_rows * n_cols)
    reordered = (
        weighted.reshape(owned, n_cols, n_rows, piece_len)
        .transpose(0, 2, 1, 3)
        .reshape(owned, reads)
    )
    row_part, col_part = (
        lax.all_to_all(weighted, ("row", "col"), split_axis=1, concat_axis=0, tiled=True),
        lax.all_to_all(reordered, ("row", "col"), split_axis=1, concat_axis=0, tiled=True),
    )
    column_reads = lax.all_gather(col_part, "row", axis=1, tiled=True)
    partial_tile = lax.dot_general(
        lax.all_gather(row_part, "col", axis=1, tiled=True),
        column_reads,
        (((0,), (0,)), ((), ())),
        preferred_element_type=jnp.float32,
    )
    row_count = partial_tile.shape[0]
    row_start = lax.axis_index("row") * row_count
    col_start = lax.axis_index("col") * partial_tile.shape[1]
    total = lax.psum(partial_tile, "layer")
    return finish(total, row_start, col_start, factor)


def solution(mesh):
    placed = (P(("row", "col", "layer"), None), P(("row", "col", "layer")), P())
    return jax.shard_map(
        body, mesh=mesh, in_specs=placed, out_specs=P("row", "col"), check_vma=False
    )
```

profile of v0, /device:TPU:1, one launch (start us, length us, event | category | flops | bytes accessed | tf_op | source)
XLA Modules:
  0.0 287.5 jit_solution(10885676402827663510)
XLA Ops:
  6.5 0.0 all-gather.5.cloned.1.call-start
  6.5 0.7 convert_bitcast_fusion
  7.2 0.1 broadcast_bitcast_fusion
  7.3 1.1 multiply_convert_fusion
  8.4 0.6 reshape.14
  9.1 0.1 copy.9
  9.2 0.3 copy.10
  9.6 52.5 %all_to_all.38 = bf16[16,128,80]{2,0,1:T(8,128)(2,1)S(1)} all-to-all(bf16[16,128,80]{2,0,1:T(8,128)(2,1)S(1)} %copy.10), channel_id=1, replica_groups=mesh['row'=8,'col'=16,'layer'=4] {'row','col'}, dimensions={1} | all-to-all | bytes 655360 | tf_op jit(solution)/shard_map/all_to_all | solution.py:36
  62.0 0.9 copy.11
  63.0 0.0 all-gather.5.cloned.1.call-update
  63.0 0.0 all-gather.3.cloned.1.call-start
  63.0 0.6 all_to_all.28
  63.7 0.3 copy.7
  64.0 39.7 %all_to_all.39 = bf16[16,128,80]{2,0,1:T(8,128)(2,1)S(1)} all-to-all(bf16[16,128,80]{2,0,1:T(8,128)(2,1)S(1)} %copy.7), channel_id=1, replica_groups=mesh['row'=8,'col'=16,'layer'=4] {'row','col'}, dimensions={1} | all-to-all | bytes 655360 | tf_op jit(solution)/shard_map/all_to_all | solution.py:35
  103.8 0.9 copy.8
  104.7 0.0 all-gather.3.cloned.1.call-update
  104.7 0.0 all-reduce.2.cloned.1.call-start
  104.8 0.0 all-gather.5.cloned.1.call-done
  104.8 67.3 %all-gather.3.cloned.1.call-done = bf16[2048,1280]{0,1:T(8,128)(2,1)} async-done(((bf16[2048,80]{0,1:T(8,128)(2,1)}), bf16[2048,1280]{0,1:T(8,128)(2,1)}) %all-gather.3.cloned.1.call-update) | async-done | bytes 5242896 | tf_op jit(solution)/shard_map/all_gather | solution.py:40
  172.1 9.3 %fusion = f32[1280,640]{1,0:T(8,128)} fusion(bf16[2048,1280]{0,1:T(8,128)(2,1)} %all-gather.3.cloned.1.call-done, bf16[2048,640]{0,1:T(8,128)(2,1)} %all-gather.5.cloned.1.call-done), kind=kOutput, calls=%fused_computation.6 | convolution fusion | flops 3355443200 | bytes 11141120 | tf_op jit(solution)/shard_map/dot_general | solution.py:39
  181.3 0.0 all-reduce.2.cloned.1.call-update
  181.4 96.0 %all-reduce.2.cloned.1.call-done = f32[1280,640]{1,0:T(8,128)} async-done(((f32[1280,640]{1,0:T(8,128)}), f32[1280,640]{1,0:T(8,128)}) %all-reduce.2.cloned.1.call-update) | async-done | bytes 3276816 | tf_op jit(solution)/shard_map/psum | solution.py:48
  277.4 3.5 %select_convert_fusion = bf16[1280,640]{1,0:T(8,128)(2,1)} fusion(f32[1280,640]{1,0:T(8,128)} %all-reduce.2.cloned.1.call-done, s32[640]{0:T(1024)S(1)} %iota_add_fusion.1, s32[1280]{0:T(1024)S(1)} %iota_add_fusion), kind=kLoop, calls=%fused_computation | loop fusion | flops 3276800 | bytes 4922880 | tf_op jit(solution)/shard_map/convert_element_type | solution.py:12
  (2 shorter events, 0.0 us)
Async XLA Ops:
  6.5 98.3 %all-gather.5.cloned.1.call-start = ((), (), s32[]{:S(2)}) async-start(), calls=%async_computation.3 | async-start | bytes 2949120 | tf_op jit(solution)/shard_map/all_gather | solution.py:38
  63.0 109.1 %all-gather.3.cloned.1.call-start = ((), (), s32[]{:S(2)}) async-start(), calls=%async_computation.2 | async-start | bytes 5570560 | tf_op jit(solution)/shard_map/all_gather | solution.py:40
  104.7 172.7 %all-reduce.2.cloned.1.call-start = ((), (), s32[]{:S(2)}) async-start(), calls=%async_computation.4 | async-start | bytes 6553600 | tf_op jit(solution)/shard_map/psum | solution.py:48
Sparse Core Ops, SparseCore 0:
  63.1 29.0 all-gather.4
  104.9 67.1 all-gather.2
  181.5 95.8 all-reduce.1
where the time goes:
time: 288 us; the launch traced here: 287 us
  waiting for transfers between devices  163 us (57%)
  blocking collectives  92.2 us (32%)
  between operations  13.2 us (5%)
  matrix products  9.28 us (3%)
  other arithmetic  5.36 us (2%)
  local copies, waits for them, and re-layouts  4.02 us (1%)
    psum x1, waiting for transfers between devices, body(): total = lax.psum(partial_tile, 'layer')  96 us
    all_gather x1, waiting for transfers between devices, body(): lax.all_gather(row_part, 'col', axis=1, tiled=True)  67.3 us
    all_to_all x1, blocking collectives, body(): lax.all_to_all(reordered, ('row', 'col'), split_axis=1, concat_axis=0, ti...  52.5 us
    all_to_all x1, blocking collectives, body(): lax.all_to_all(weighted, ('row', 'col'), split_axis=1, concat_axis=0, til...  39.7 us
    dot_general x1, matrix products, body(): lax.dot_general(lax.all_gather(row_part, 'col', axis=1, tiled=True), colu...  9.28 us
  transfers between devices with their start and end apart: 3, of which 2 were waited for; matrix products, arithmetic and copies ran while one was open for 0% of the time, Pallas kernels for 0%

commit v1 on v0

--- a/solution.py
+++ b/solution.py
@@ -45,7 +45,9 @@
     row_count = partial_tile.shape[0]
     row_start = lax.axis_index("row") * row_count
     col_start = lax.axis_index("col") * partial_tile.shape[1]
-    total = lax.psum(partial_tile, "layer")
+    total = partial_tile
+    for hop in (1, 2):
+        total = total + lax.ppermute(total, "layer", [(dev, dev ^ hop) for dev in range(4)])
     return finish(total, row_start, col_start, factor)
 
 

time: 288 us -> 336 us (1.17); the launches traced: 287 us -> 329 us
  waiting for transfers between devices: 163 us -> 200 us
  starting transfers between devices: 0.09 us -> 6.96 us
    ppermute x0 -> x2, waiting for transfers between devices: none -> 133 us  [body(): lax.ppermute(total, 'layer', [(dev, dev ^ hop) for dev in range(4)])]
    psum x1 -> x0, waiting for transfers between devices: 96 us -> none  [body(): total = lax.psum(partial_tile, 'layer')]
    ppermute x0 -> x2, starting transfers between devices: none -> 6.91 us  [body(): lax.ppermute(total, 'layer', [(dev, dev ^ hop) for dev in range(4)])]
  transfers between devices with their start and end apart: 3 -> 4, of which waited for: 2 -> 3; matrix products, arithmetic and copies ran while one was open for 0% -> 0% of each run, Pallas kernels for 0% -> 0%
where the time goes in v1:
time: 336 us; the launch traced here: 329 us
  waiting for transfers between devices  200 us (60%)
  blocking collectives  92.2 us (27%)
  between operations  13.5 us (4%)
  matrix products  7.02 us (2%)
  starting transfers between devices  6.96 us (2%)
  other arithmetic  5.78 us (2%)
  local copies, waits for them, and re-layouts  4 us (1%)
    ppermute x2, waiting for transfers between devices, body(): lax.ppermute(total, 'layer', [(dev, dev ^ hop) for dev in range(4)])  133 us
    all_gather x1, waiting for transfers between devices, body(): lax.all_gather(row_part, 'col', axis=1, tiled=True)  67.3 us
    all_to_all x1, blocking collectives, body(): lax.all_to_all(reordered, ('row', 'col'), split_axis=1, concat_axis=0, ti...  52.5 us
    all_to_all x1, blocking collectives, body(): lax.all_to_all(weighted, ('row', 'col'), split_axis=1, concat_axis=0, til...  39.7 us
    dot_general x1, matrix products, body(): lax.dot_general(lax.all_gather(row_part, 'col', axis=1, tiled=True), colu...  7.02 us
    ppermute x2, starting transfers between devices, body(): lax.ppermute(total, 'layer', [(dev, dev ^ hop) for dev in range(4)])  6.91 us
  transfers between devices with their start and end apart: 4, of which 3 were waited for; matrix products, arithmetic and copies ran while one was open for 0% of the time, Pallas kernels for 0%

profile of v1, /device:TPU:1, one launch (start us, length us, event | category | flops | bytes accessed | tf_op | source)
XLA Modules:
  0.0 329.5 jit_solution(16987578631194736360)
XLA Ops:
  6.5 0.0 all-gather.5.cloned.1.call-start
  6.5 0.7 convert_bitcast_fusion
  7.2 0.1 broadcast_bitcast_fusion
  7.3 1.1 multiply_convert_fusion
  8.4 0.6 reshape.14
  9.1 0.1 copy.9
  9.2 0.3 copy.10
  9.6 52.5 %all_to_all.38 = bf16[16,128,80]{2,0,1:T(8,128)(2,1)S(1)} all-to-all(bf16[16,128,80]{2,0,1:T(8,128)(2,1)S(1)} %copy.10), channel_id=1, replica_groups=mesh['row'=8,'col'=16,'layer'=4] {'row','col'}, dimensions={1} | all-to-all | bytes 655360 | tf_op jit(solution)/shard_map/all_to_all | solution.py:36
  62.0 0.9 copy.11
  63.0 0.0 all-gather.5.cloned.1.call-update
  63.0 0.0 all-gather.3.cloned.1.call-start
  63.0 0.6 all_to_all.28
  63.7 0.3 copy.7
  64.0 39.7 %all_to_all.39 = bf16[16,128,80]{2,0,1:T(8,128)(2,1)S(1)} all-to-all(bf16[16,128,80]{2,0,1:T(8,128)(2,1)S(1)} %copy.7), channel_id=1, replica_groups=mesh['row'=8,'col'=16,'layer'=4] {'row','col'}, dimensions={1} | all-to-all | bytes 655360 | tf_op jit(solution)/shard_map/all_to_all | solution.py:35
  103.8 0.9 copy.8
  104.7 0.0 all-gather.3.cloned.1.call-update
  104.7 0.0 all-gather.5.cloned.1.call-done
  104.7 67.3 %all-gather.3.cloned.1.call-done = bf16[2048,1280]{0,1:T(8,128)(2,1)} async-done(((bf16[2048,80]{0,1:T(8,128)(2,1)}), bf16[2048,1280]{0,1:T(8,128)(2,1)}) %all-gather.3.cloned.1.call-update) | async-done | bytes 5242896 | tf_op jit(solution)/shard_map/all_gather | solution.py:40
  172.0 7.0 %fusion = f32[1280,640]{1,0:T(8,128)S(1)} fusion(bf16[2048,1280]{0,1:T(8,128)(2,1)} %all-gather.3.cloned.1.call-done, bf16[2048,640]{0,1:T(8,128)(2,1)} %all-gather.5.cloned.1.call-done), kind=kOutput, calls=%fused_computation.6 | convolution fusion | flops 3355443200 | bytes 11141120 | tf_op jit(solution)/shard_map/dot_general | solution.py:39
  179.1 2.8 collective-permute-start
  181.9 64.5 %collective-permute-done = f32[1280,640]{1,0:T(8,128)S(1)} collective-permute-done((f32[1280,640]{1,0:T(8,128)S(1)}, f32[1280,640]{1,0:T(8,128)S(1)}, u32[]{:S(2)}, u32[]{:S(2)}) %collective-permute-start) | collective-permute-done | bytes 3276832 | tf_op jit(solution)/shard_map/ppermute | solution.py:50
  246.4 0.3 add.37
  246.7 4.1 %collective-permute-start.1 = (f32[1280,640]{1,0:T(8,128)S(1)}, f32[1280,640]{1,0:T(8,128)}, u32[]{:S(2)}, u32[]{:S(2)}) collective-permute-start(f32[1280,640]{1,0:T(8,128)S(1)} %add.37), channel_id=1, source_target_pairs={{0,2},{1,3},{2,0},{3,1},{4,6},{5,7},{6,4},{7,5},{8,10},{9,11},{10,... | collective-permute-start | bytes 9830408 | tf_op jit(solution)/shard_map/ppermute | solution.py:50
  250.8 68.2 %collective-permute-done.1 = f32[1280,640]{1,0:T(8,128)} collective-permute-done((f32[1280,640]{1,0:T(8,128)S(1)}, f32[1280,640]{1,0:T(8,128)}, u32[]{:S(2)}, u32[]{:S(2)}) %collective-permute-start.1) | collective-permute-done | bytes 3276832 | tf_op jit(solution)/shard_map/ppermute | solution.py:50
  319.0 3.6 %select_convert_fusion = bf16[1280,640]{1,0:T(8,128)(2,1)} fusion(f32[1280,640]{1,0:T(8,128)S(1)} %add.37, f32[1280,640]{1,0:T(8,128)} %collective-permute-done.1, s32[640]{0:T(1024)S(1)} %iota_add_fusion.1, s32[1280]{0:T(1024)S(1)} %iota_add_fusion), kind=kLoop, calls=%fused_computation | loop fusion | flops 4096000 | bytes 8199680 | tf_op jit(solution)/shard_map/convert_element_type | solution.py:12
  (2 shorter events, 0.0 us)
Async XLA Ops:
  6.5 98.2 %all-gather.5.cloned.1.call-start = ((), (), s32[]{:S(2)}) async-start(), calls=%async_computation.3 | async-start | bytes 2949120 | tf_op jit(solution)/shard_map/all_gather | solution.py:38
  63.0 109.1 %all-gather.3.cloned.1.call-start = ((), (), s32[]{:S(2)}) async-start(), calls=%async_computation.2 | async-start | bytes 5570560 | tf_op jit(solution)/shard_map/all_gather | solution.py:40
  179.1 67.3 %collective-permute-start = (f32[1280,640]{1,0:T(8,128)S(1)}, f32[1280,640]{1,0:T(8,128)S(1)}, u32[]{:S(2)}, u32[]{:S(2)}) collective-permute-start(f32[1280,640]{1,0:T(8,128)S(1)} %fusion), channel_id=1, source_target_pairs={{0,1},{1,0},{2,3},{3,2},{4,5},{5,4},{6,7},{7,6},{8,9},{9,8},{10,11... | collective-permute-start | bytes 9830408 | tf_op jit(solution)/shard_map/ppermute | solution.py:50
  246.7 72.3 %collective-permute-start.1 = (f32[1280,640]{1,0:T(8,128)S(1)}, f32[1280,640]{1,0:T(8,128)}, u32[]{:S(2)}, u32[]{:S(2)}) collective-permute-start(f32[1280,640]{1,0:T(8,128)S(1)} %add.37), channel_id=1, source_target_pairs={{0,2},{1,3},{2,0},{3,1},{4,6},{5,7},{6,4},{7,5},{8,10},{9,11},{10,... | collective-permute-start | bytes 9830408 | tf_op jit(solution)/shard_map/ppermute | solution.py:50
Sparse Core Ops, SparseCore 0:
  63.1 29.0 all-gather.4
  104.8 67.1 all-gather.2
